TPU v7x, 32 devices: a whole 2x2x4 slice. The times are simulated.
32 devices in a mesh: dp: 4 (over y, x), tensor: 8 (over z, core).
Axes of the slice: x: 2, y: 2, z: 4, core: 2. Of those that a mesh axis runs over, the one named last changes fastest.
Arguments:
- latents: bfloat16 [4, 2048, 1152], P('dp', 'tensor'), may hold values from -6 to 6
- conditioning: bfloat16 [4, 1152], P('dp', 'tensor'), may hold values from -6 to 6
- ada_weight: bfloat16 [2, 1152, 6912], P(None, 'tensor'), may hold values from -0.1875 to 0.1875
- ada_bias: bfloat16 [2, 6912], replicated, may hold values from -3 to 3
- qkv_weight: bfloat16 [2, 1152, 3, 1152], P(None, None, None, 'tensor'), may hold values from -0.1875 to 0.1875
- qkv_bias: bfloat16 [2, 2, 1152], P(None, None, 'tensor'), may hold values from -3 to 3
- out_weight: bfloat16 [2, 1152, 1152], P(None, 'tensor'), may hold values from -0.75 to 0.75
- out_bias: bfloat16 [2, 1152], replicated, may hold values from -3 to 3
- fc1_weight: bfloat16 [2, 1152, 4608], P(None, None, 'tensor'), may hold values from -0.1875 to 0.1875
- fc1_bias: bfloat16 [2, 4608], P(None, 'tensor'), may hold values from -3 to 3
- fc2_weight: bfloat16 [2, 4608, 1152], P(None, 'tensor'), may hold values from -0.09375 to 0.09375
- fc2_bias: bfloat16 [2, 1152], replicated, may hold values from -3 to 3
- out_grad: bfloat16 [4, 2048, 1152], P('dp', 'tensor'), may hold values from -6 to 6
Outputs:
- layer_output: bfloat16 [4, 2048, 1152], P('dp', 'tensor')
- latents_grad: bfloat16 [4, 2048, 1152], P('dp', 'tensor')
- conditioning_grad: bfloat16 [4, 1152], P('dp', 'tensor')
- ada_weight_grad: float32 [2, 1152, 6912], P(None, 'tensor')
- ada_bias_grad: float32 [2, 6912], replicated
- qkv_weight_grad: float32 [2, 1152, 3, 1152], P(None, None, None, 'tensor')
- qkv_bias_grad: float32 [2, 2, 1152], P(None, None, 'tensor')
- out_weight_grad: float32 [2, 1152, 1152], P(None, 'tensor')
- out_bias_grad: float32 [2, 1152], replicated
- fc1_weight_grad: float32 [2, 1152, 4608], P(None, None, 'tensor')
- fc1_bias_grad: float32 [2, 4608], P(None, 'tensor')
- fc2_weight_grad: float32 [2, 4608, 1152], P(None, 'tensor')
- fc2_bias_grad: float32 [2, 1152], replicated
All inputs are finite; a program needn't handle non-finite values.
Results may differ from a plain program's by a relative error of at most 0.04.
Values may be sent and summed in bfloat16 or wider, within the bound.
A program may use at most 256 MiB of HBM per device.

v0:
```python
from functools import partial
import jax
import jax.numpy as jnp
from jax import lax
from jax.sharding import PartitionSpec as P

HEAD_DIM = 72
PATCHES = 256
FRAMES = 8
LAYERS = 2


def normalize(stream):
    centered = stream - jnp.mean(stream, axis=-1, keepdims=True)
    variance = jnp.mean(centered * centered, axis=-1, keepdims=True)
    return centered * lax.rsqrt(variance + 1e-06)


def modulate(stream, shift_in, scale_in):
    return normalize(stream) * (1.0 + scale_in) + shift_in


def grouped(token_rows, spatial):
    heads_here = token_rows.shape[1] // HEAD_DIM
    shaped = token_rows.reshape(FRAMES, PATCHES, heads_here, HEAD_DIM)
    if spatial:
        return shaped
    return jnp.transpose(shaped, (1, 0, 2, 3))


def ungrouped(groups, spatial):
    if not spatial:
        groups = jnp.transpose(groups, (1, 0, 2, 3))
    return groups.reshape(FRAMES * PATCHES, groups.shape[2] * HEAD_DIM)


def softmax_rows(query_g, key_g):
    scores = jnp.einsum(
        "gqhd,gkhd->ghqk", query_g, key_g, preferred_element_type=jnp.float32
    ) * HEAD_DIM ** (-0.5)
    return jax.nn.softmax(scores, axis=-1)


def attend(query_rows, key_rows, value_rows, spatial):
    attn_probs = softmax_rows(grouped(query_rows, spatial), grouped(key_rows, spatial)).astype(
        jnp.bfloat16
    )
    mixed = jnp.einsum(
        "ghqk,gkhd->gqhd",
        attn_probs,
        grouped(value_rows, spatial),
        preferred_element_type=jnp.float32,
    )
    return ungrouped(mixed, spatial)


def attend_back(query_rows, key_rows, value_rows, mixed_grad, spatial):
    query_g = grouped(query_rows, spatial)
    key_g = grouped(key_rows, spatial)
    value_g = grouped(value_rows, spatial)
    grad_g = grouped(mixed_grad, spatial)
    probs_full = softmax_rows(query_g, key_g)
    value_grad = jnp.einsum(
        "ghqk,gqhd->gkhd",
        probs_full.astype(jnp.bfloat16),
        grad_g,
        preferred_element_type=jnp.float32,
    )
    probs_grad = jnp.einsum("gqhd,gkhd->ghqk", grad_g, value_g, preferred_element_type=jnp.float32)
    score_grad = probs_full * (
        probs_grad - jnp.sum(probs_grad * probs_full, axis=-1, keepdims=True)
    )
    score_low = score_grad.astype(jnp.bfloat16)
    factor = HEAD_DIM ** (-0.5)
    query_grad = (
        jnp.einsum("ghqk,gkhd->gqhd", score_low, key_g, preferred_element_type=jnp.float32) * factor
    )
    key_grad = (
        jnp.einsum("ghqk,gqhd->gkhd", score_low, query_g, preferred_element_type=jnp.float32)
        * factor
    )
    return (
        ungrouped(query_grad, spatial),
        ungrouped(key_grad, spatial),
        ungrouped(value_grad, spatial),
    )


def spread_rows(row_block):
    return lax.all_gather(row_block, "tensor", axis=0, tiled=True)


def reduce_rows(partial_terms):
    return lax.psum_scatter(
        partial_terms.astype(jnp.bfloat16), "tensor", scatter_dimension=0, tiled=True
    ).astype(jnp.float32)


def spread_grads(row_block):
    return lax.all_gather(row_block, "tensor", axis=0, tiled=True)


def reduce_grads(partial_terms):
    return lax.psum_scatter(
        partial_terms.astype(jnp.bfloat16), "tensor", scatter_dimension=0, tiled=True
    ).astype(jnp.float32)


def layer_forward(stream, modulation, params, spatial):
    qkv_w, qkv_b, out_w, out_b, fc1_w, fc1_b, fc2_w, fc2_b = params
    shift_att, scale_att, gate_att, shift_mlp, scale_mlp, gate_mlp = jnp.split(modulation, 6)
    normed = spread_rows(modulate(stream, shift_att, scale_att).astype(jnp.bfloat16))
    head_width = qkv_w.shape[2]
    projected = jnp.dot(
        normed, qkv_w.reshape(qkv_w.shape[0], 3 * head_width), preferred_element_type=jnp.float32
    )
    query_rows = (projected[:, :head_width] + qkv_b[0].astype(jnp.float32)).astype(jnp.bfloat16)
    key_rows = projected[:, head_width : 2 * head_width].astype(jnp.bfloat16)
    value_rows = (projected[:, 2 * head_width :] + qkv_b[1].astype(jnp.float32)).astype(
        jnp.bfloat16
    )
    heads_out = attend(query_rows, key_rows, value_rows, spatial).astype(jnp.bfloat16)
    attn_branch = reduce_rows(
        jnp.dot(heads_out, out_w, preferred_element_type=jnp.float32)
    ) + out_b.astype(jnp.float32)
    middle = stream + gate_att * attn_branch
    normed_mlp = spread_rows(modulate(middle, shift_mlp, scale_mlp).astype(jnp.bfloat16))
    hidden = jnp.dot(normed_mlp, fc1_w, preferred_element_type=jnp.float32) + fc1_b.astype(
        jnp.float32
    )
    activated = jax.nn.gelu(hidden, approximate=True).astype(jnp.bfloat16)
    mlp_branch = reduce_rows(
        jnp.dot(activated, fc2_w, preferred_element_type=jnp.float32)
    ) + fc2_b.astype(jnp.float32)
    result = middle + gate_mlp * mlp_branch
    saved = (
        normed,
        query_rows,
        key_rows,
        value_rows,
        heads_out,
        attn_branch,
        middle,
        normed_mlp,
        hidden,
        mlp_branch,
    )
    return (result, saved)


def layer_backward(stream, modulation, params, saved, stream_grad, spatial):
    qkv_w, qkv_b, out_w, out_b, fc1_w, fc1_b, fc2_w, fc2_b = params
    (
        normed,
        query_rows,
        key_rows,
        value_rows,
        heads_out,
        attn_branch,
        middle,
        normed_mlp,
        hidden,
        mlp_branch,
    ) = saved
    shift_att, scale_att, gate_att, shift_mlp, scale_mlp, gate_mlp = jnp.split(modulation, 6)
    head_width = qkv_w.shape[2]
    mlp_grad = (gate_mlp * stream_grad).astype(jnp.bfloat16)
    gate_mlp_grad = jnp.sum(stream_grad * mlp_branch, axis=0)
    fc2_b_grad = jnp.sum(mlp_grad, axis=0, dtype=jnp.float32)
    mlp_grad_all = spread_grads(mlp_grad)
    gelu_out, gelu_back = jax.vjp(partial(jax.nn.gelu, approximate=True), hidden)
    activated = gelu_out.astype(jnp.bfloat16)
    fc2_w_grad = jnp.einsum(
        "tf,td->fd", activated, mlp_grad_all, preferred_element_type=jnp.float32
    )
    act_grad = jnp.einsum("td,fd->tf", mlp_grad_all, fc2_w, preferred_element_type=jnp.float32)
    hidden_grad = gelu_back(act_grad)[0].astype(jnp.bfloat16)
    fc1_b_grad = jnp.sum(hidden_grad, axis=0, dtype=jnp.float32)
    fc1_w_grad = jnp.einsum(
        "td,tf->df", normed_mlp, hidden_grad, preferred_element_type=jnp.float32
    )
    mlp_in_grad = reduce_grads(
        jnp.einsum("tf,df->td", hidden_grad, fc1_w, preferred_element_type=jnp.float32)
    )
    _, mlp_norm_back = jax.vjp(modulate, middle, shift_mlp, scale_mlp)
    middle_part, shift_mlp_grad, scale_mlp_grad = mlp_norm_back(mlp_in_grad)
    middle_grad = stream_grad + middle_part
    attn_grad = (gate_att * middle_grad).astype(jnp.bfloat16)
    gate_att_grad = jnp.sum(middle_grad * attn_branch, axis=0)
    out_b_grad = jnp.sum(attn_grad, axis=0, dtype=jnp.float32)
    attn_grad_all = spread_grads(attn_grad)
    out_w_grad = jnp.einsum(
        "tw,td->wd", heads_out, attn_grad_all, preferred_element_type=jnp.float32
    )
    heads_grad = jnp.einsum(
        "td,wd->tw", attn_grad_all, out_w, preferred_element_type=jnp.float32
    ).astype(jnp.bfloat16)
    query_grad, key_grad, value_grad = attend_back(
        query_rows, key_rows, value_rows, heads_grad, spatial
    )
    qkv_grad = jnp.concatenate([query_grad, key_grad, value_grad], axis=1).astype(jnp.bfloat16)
    qkv_b_grad = jnp.stack(
        [
            jnp.sum(qkv_grad[:, :head_width], axis=0, dtype=jnp.float32),
            jnp.sum(qkv_grad[:, 2 * head_width :], axis=0, dtype=jnp.float32),
        ]
    )
    qkv_flat = qkv_w.reshape(qkv_w.shape[0], 3 * head_width)
    qkv_w_grad = jnp.einsum(
        "td,tw->dw", normed, qkv_grad, preferred_element_type=jnp.float32
    ).reshape(qkv_w.shape)
    attn_in_grad = reduce_grads(
        jnp.einsum("tw,dw->td", qkv_grad, qkv_flat, preferred_element_type=jnp.float32)
    )
    _, att_norm_back = jax.vjp(modulate, stream, shift_att, scale_att)
    stream_part, shift_att_grad, scale_att_grad = att_norm_back(attn_in_grad)
    input_grad = middle_grad + stream_part
    modulation_grad = jnp.concatenate(
        [
            shift_att_grad,
            scale_att_grad,
            gate_att_grad,
            shift_mlp_grad,
            scale_mlp_grad,
            gate_mlp_grad,
        ]
    )
    return (
        input_grad,
        modulation_grad,
        (
            qkv_w_grad,
            qkv_b_grad,
            out_w_grad,
            out_b_grad,
            fc1_w_grad,
            fc1_b_grad,
            fc2_w_grad,
            fc2_b_grad,
        ),
    )


def per_device(
    latents,
    conditioning,
    ada_weight,
    ada_bias,
    qkv_weight,
    qkv_bias,
    out_weight,
    out_bias,
    fc1_weight,
    fc1_bias,
    fc2_weight,
    fc2_bias,
    out_grad,
):
    cond_row = conditioning[0].astype(jnp.float32)
    silu_out, silu_back = jax.vjp(jax.nn.silu, cond_row)
    silu_cond = silu_out.astype(jnp.bfloat16)
    ada_terms = jnp.einsum("d,ldm->lm", silu_cond, ada_weight, preferred_element_type=jnp.float32)
    modulations = lax.psum(ada_terms, "tensor") + ada_bias.astype(jnp.float32)
    stacked = (
        qkv_weight,
        qkv_bias,
        out_weight,
        out_bias,
        fc1_weight,
        fc1_bias,
        fc2_weight,
        fc2_bias,
    )
    stream = latents[0].astype(jnp.float32)
    inputs_kept = []
    saved_all = []
    for layer_idx in range(LAYERS):
        params = tuple((member[layer_idx] for member in stacked))
        inputs_kept.append(stream)
        stream, saved = layer_forward(stream, modulations[layer_idx], params, layer_idx % 2 == 0)
        saved_all.append(saved)
    layer_output = stream.astype(jnp.bfloat16)[None]
    stream_grad = out_grad[0].astype(jnp.float32)
    mod_grads = [None] * LAYERS
    layer_grads = [None] * LAYERS
    for layer_idx in reversed(range(LAYERS)):
        params = tuple((member[layer_idx] for member in stacked))
        spatial = layer_idx % 2 == 0
        saved = layer_forward(inputs_kept[layer_idx], modulations[layer_idx], params, spatial)[1]
        stream_grad, mod_grads[layer_idx], layer_grads[layer_idx] = layer_backward(
            inputs_kept[layer_idx], modulations[layer_idx], params, saved, stream_grad, spatial
        )

    def collect(position):
        return jnp.stack([member[position] for member in layer_grads])

    mod_sum, out_b_sum, fc2_b_sum = (
        lax.psum(jnp.stack(mod_grads).astype(jnp.bfloat16), "tensor").astype(jnp.float32),
        lax.psum(collect(3).astype(jnp.bfloat16), "tensor").astype(jnp.float32),
        lax.psum(collect(7).astype(jnp.bfloat16), "tensor").astype(jnp.float32),
    )
    mod_low = mod_sum.astype(jnp.bfloat16)
    ada_w_grad = (
        silu_cond.astype(jnp.float32)[None, :, None] * mod_low.astype(jnp.float32)[:, None, :]
    )
    ada_b_grad = mod_low.astype(jnp.float32)
    silu_grad = jnp.einsum("lm,ldm->d", mod_low, ada_weight, preferred_element_type=jnp.float32)
    cond_grad = silu_back(silu_grad)[0]
    summed = (
        lax.psum(ada_w_grad.astype(jnp.bfloat16), "dp").astype(jnp.float32),
        lax.psum(ada_b_grad.astype(jnp.bfloat16), "dp").astype(jnp.float32),
        lax.psum(collect(0).astype(jnp.bfloat16), "dp").astype(jnp.float32),
        lax.psum(collect(1).astype(jnp.bfloat16), "dp").astype(jnp.float32),
        lax.psum(collect(2).astype(jnp.bfloat16), "dp").astype(jnp.float32),
        lax.psum(out_b_sum.astype(jnp.bfloat16), "dp").astype(jnp.float32),
        lax.psum(collect(4).astype(jnp.bfloat16), "dp").astype(jnp.float32),
        lax.psum(collect(5).astype(jnp.bfloat16), "dp").astype(jnp.float32),
        lax.psum(collect(6).astype(jnp.bfloat16), "dp").astype(jnp.float32),
        lax.psum(fc2_b_sum.astype(jnp.bfloat16), "dp").astype(jnp.float32),
    )
    return (
        layer_output,
        stream_grad.astype(jnp.bfloat16)[None],
        cond_grad.astype(jnp.bfloat16)[None],
        summed[0],
        summed[1],
        summed[2],
        summed[3],
        summed[4],
        summed[5],
        summed[6],
        summed[7],
        summed[8],
        summed[9],
    )


def solution(mesh):
    in_specs = (
        P("dp", "tensor", None),
        P("dp", "tensor"),
        P(None, "tensor", None),
        P(),
        P(None, None, None, "tensor"),
        P(None, None, "tensor"),
        P(None, "tensor", None),
        P(),
        P(None, None, "tensor"),
        P(None, "tensor"),
        P(None, "tensor", None),
        P(),
        P("dp", "tensor", None),
    )
    out_specs = (
        P("dp", "tensor", None),
        P("dp", "tensor", None),
        P("dp", "tensor"),
        P(None, "tensor", None),
        P(),
        P(None, None, None, "tensor"),
        P(None, None, "tensor"),
        P(None, "tensor", None),
        P(),
        P(None, None, "tensor"),
        P(None, "tensor"),
        P(None, "tensor", None),
        P(),
    )
    return jax.shard_map(
        per_device, mesh=mesh, in_specs=in_specs, out_specs=out_specs, check_vma=False
    )
```

profile of v0, /device:TPU:0, one launch (start us, length us, event | category | flops | bytes accessed | tf_op | source)
XLA Modules:
  0.0 1360.1 jit_solution(16830422912774858308)
XLA Ops:
  11.1 2.8 fusion.180
  14.0 30.9 %psum.98 = f32[2,6912]{1,0:T(2,128)S(1)} all-reduce(f32[2,6912]{1,0:T(2,128)S(1)} %bitcast.362), channel_id=1, replica_groups=mesh['dp'=4,'tensor'=8] {'tensor'}, use_global_device_ids=true, to_apply=%region_0.1 | all-reduce | flops 13824 | bytes 110592 | tf_op jit(solution)/shard_map/psum | solution.py:263
  48.3 48.6 %all-gather.9.cloned.1.call-done = bf16[2048,1152]{1,0:T(8,128)(2,1)} async-done(((bf16[256,1152]{1,0:T(8,128)(2,1)}), bf16[2048,1152]{1,0:T(8,128)(2,1)}) %all-gather.9.cloned.1.call-update) | async-done | bytes 4718608 | tf_op jit(solution)/shard_map/all_gather | solution.py:90
  96.8 5.1 fusion.181
  104.4 3.2 fusion.168
  110.7 3.8 convolution_convert_fusion.7
  115.8 52.6 %reduce-scatter.9.cloned.1.call-done = bf16[256,1152]{1,0:T(8,128)(2,1)} async-done(((bf16[2048,1152]{1,0:T(8,128)(2,1)}), bf16[256,1152]{1,0:T(8,128)(2,1)}) %reduce-scatter.9.cloned.1.call-update) | async-done | bytes 589840 | tf_op jit(solution)/shard_map/reduce_scatter | solution.py:94
  173.6 49.3 %all-gather.11.cloned.1.call-done = bf16[2048,1152]{1,0:T(8,128)(2,1)} async-done(((bf16[256,1152]{1,0:T(8,128)(2,1)}), bf16[2048,1152]{1,0:T(8,128)(2,1)}) %all-gather.11.cloned.1.call-update) | async-done | bytes 4718608 | tf_op jit(solution)/shard_map/all_gather | solution.py:90
  223.0 5.6 fusion.59
  228.7 2.2 copy-done.121
  230.9 6.7 convolution_convert_fusion.6
  238.9 52.6 %reduce-scatter.11.cloned.1.call-done = bf16[256,1152]{1,0:T(8,128)(2,1)} async-done(((bf16[2048,1152]{1,0:T(8,128)(2,1)}), bf16[256,1152]{1,0:T(8,128)(2,1)}) %reduce-scatter.11.cloned.1.call-update) | async-done | bytes 589840 | tf_op jit(solution)/shard_map/reduce_scatter | solution.py:94
  294.5 50.2 %all-gather.13.cloned.1.call-done = bf16[2048,1152]{1,0:T(8,128)(2,1)} async-done(((bf16[256,1152]{1,0:T(8,128)(2,1)}), bf16[2048,1152]{1,0:T(8,128)(2,1)}) %all-gather.13.cloned.1.call-update) | async-done | bytes 4718608 | tf_op jit(solution)/shard_map/all_gather | solution.py:90
  344.7 4.8 fusion.182
  356.7 5.3 fusion.169
  362.0 3.7 fusion.40
  368.6 4.8 convolution_convert_fusion.5
  373.4 53.9 %reduce-scatter.13.cloned.1.call-done = bf16[256,1152]{1,0:T(8,128)(2,1)} async-done(((bf16[2048,1152]{1,0:T(8,128)(2,1)}), bf16[256,1152]{1,0:T(8,128)(2,1)}) %reduce-scatter.13.cloned.1.call-update) | async-done | bytes 589840 | tf_op jit(solution)/shard_map/reduce_scatter | solution.py:94
  431.9 2.6 fusion.159
  435.0 47.1 %all-gather.15.cloned.1.call-done = bf16[2048,1152]{1,0:T(8,128)(2,1)} async-done(((bf16[256,1152]{1,0:T(8,128)(2,1)}), bf16[2048,1152]{1,0:T(8,128)(2,1)}) %all-gather.15.cloned.1.call-update) | async-done | bytes 4718608 | tf_op jit(solution)/shard_map/all_gather | solution.py:90
  482.1 8.2 fusion.51
  490.2 44.6 %all-gather.17.cloned.1.call-done = bf16[2048,1152]{1,0:T(8,128)(2,1)} async-done(((bf16[256,1152]{1,0:T(8,128)(2,1)}), bf16[2048,1152]{1,0:T(8,128)(2,1)}) %all-gather.17.cloned.1.call-update) | async-done | bytes 4718608 | tf_op jit(solution)/shard_map/all_gather | solution.py:100
  534.8 9.9 fusion.178
  546.2 5.8 convolution_convert_fusion.3
  552.2 10.0 convolution_convert_fusion.4
  562.3 43.6 %reduce-scatter.17.cloned.1.call-done = bf16[256,1152]{1,0:T(8,128)(2,1)} async-done(((bf16[2048,1152]{1,0:T(8,128)(2,1)}), bf16[256,1152]{1,0:T(8,128)(2,1)}) %reduce-scatter.17.cloned.1.call-update) | async-done | bytes 589840 | tf_op jit(solution)/shard_map/reduce_scatter | solution.py:104
  605.9 2.1 fusion.74
  609.3 52.7 %reduce-scatter.15.cloned.1.call-done = bf16[256,1152]{1,0:T(8,128)(2,1)} async-done(((bf16[2048,1152]{1,0:T(8,128)(2,1)}), bf16[256,1152]{1,0:T(8,128)(2,1)}) %reduce-scatter.15.cloned.1.call-update) | async-done | bytes 589840 | tf_op jit(solution)/shard_map/reduce_scatter | solution.py:94
  662.0 2.7 fusion.164
  667.7 50.0 %all-gather.19.cloned.1.call-done = bf16[2048,1152]{1,0:T(8,128)(2,1)} async-done(((bf16[256,1152]{1,0:T(8,128)(2,1)}), bf16[2048,1152]{1,0:T(8,128)(2,1)}) %all-gather.19.cloned.1.call-update) | async-done | bytes 4718608 | tf_op jit(solution)/shard_map/all_gather | solution.py:100
  717.7 4.0 convolution_convert_fusion.17
  723.7 4.3 fusion.174
  731.7 2.3 fusion.175
  744.6 4.6 convolution_convert_fusion.1
  749.3 53.9 %reduce-scatter.19.cloned.1.call-done = bf16[256,1152]{1,0:T(8,128)(2,1)} async-done(((bf16[2048,1152]{1,0:T(8,128)(2,1)}), bf16[256,1152]{1,0:T(8,128)(2,1)}) %reduce-scatter.19.cloned.1.call-update) | async-done | bytes 589840 | tf_op jit(solution)/shard_map/reduce_scatter | solution.py:104
  805.2 2.2 fusion.75
  807.6 2.5 fusion.158
  810.4 49.9 %all-gather.21.cloned.1.call-done = bf16[2048,1152]{1,0:T(8,128)(2,1)} async-done(((bf16[256,1152]{1,0:T(8,128)(2,1)}), bf16[2048,1152]{1,0:T(8,128)(2,1)}) %all-gather.21.cloned.1.call-update) | async-done | bytes 4718608 | tf_op jit(solution)/shard_map/all_gather | solution.py:100
  860.3 9.9 fusion.179
  871.6 5.8 convolution_convert_fusion.2
  877.5 53.9 %reduce-scatter.21.cloned.1.call-done = bf16[256,1152]{1,0:T(8,128)(2,1)} async-done(((bf16[2048,1152]{1,0:T(8,128)(2,1)}), bf16[256,1152]{1,0:T(8,128)(2,1)}) %reduce-scatter.21.cloned.1.call-update) | async-done | bytes 589840 | tf_op jit(solution)/shard_map/reduce_scatter | solution.py:104
  931.4 2.4 fusion.76
  937.0 49.7 %all-gather.23.cloned.1.call-done = bf16[2048,1152]{1,0:T(8,128)(2,1)} async-done(((bf16[256,1152]{1,0:T(8,128)(2,1)}), bf16[2048,1152]{1,0:T(8,128)(2,1)}) %all-gather.23.cloned.1.call-update) | async-done | bytes 4718608 | tf_op jit(solution)/shard_map/all_gather | solution.py:100
  986.8 4.1 convolution_convert_fusion.16
  999.2 4.6 convolution_convert_fusion
  1005.0 7.3 fusion.22
  1012.4 9.2 fusion.20
  1024.0 2.6 fusion.79
  1026.6 3.5 fusion.24
  1030.2 5.9 convolution_convert_fusion.12
  1038.2 6.4 fusion.21
  1046.4 8.2 fusion.19
  1056.7 3.5 fusion.23
  1061.1 4.9 convolution_convert_fusion.13
  1074.2 26.9 %all-reduce = (bf16[2,6912]{1,0:T(2,128)(2,1)S(1)}, bf16[2,1152]{1,0:T(2,128)(2,1)S(1)}, bf16[2,1152]{1,0:T(2,128)(2,1)S(1)}) all-reduce(bf16[2,6912]{1,0:T(2,128)(2,1)S(1)} %pad_maximum_fusion.4, bf16[2,1152]{1,0:T(2,128)(2,1)S(1)} %get-tuple-element.108, ...), channel_id=1, replica_groups=mesh['dp'=4,'tensor'=8] {'tensor'}, use_global_device_ids=true, to_apply=%region_43.44 | all-reduce | flops 18432 | bytes 73728 | tf_op jit(solution)/shard_map/psum | solution.py:298
  1101.1 2.5 multiply_convert_fusion
  1104.6 3.2 fusion.128
  1108.5 18.3 %all-reduce.1 = (bf16[2,6912]{1,0:T(2,128)(2,1)S(1)}, bf16[2,2,144]{2,1,0:T(2,128)(2,1)S(1)}, bf16[2,1152]{1,0:T(2,128)(2,1)S(1)}, bf16[2,576]{1,0:T(2,128)(2,1)S(1)}, bf16[2,1152]{1,0:T(2,128)(2,1)S(1)}) all-reduce(bf16[2,6912]{1,0:T(2,128)(2,1)S(1)} %get-tuple-element.41, ...), channel_id=1, replica_groups=mesh['dp'=4,'tensor'=8] {'dp'}, use_global_device_ids=true, to_apply=%region_45.46 | all-reduce | flops 20160 | bytes 80640 | tf_op jit(solution)/shard_map/psum | solution.py:311
  1129.9 206.3 %all-reduce.5.cloned.1.call-done = (bf16[2,144,6912]{2,1,0:T(8,128)(2,1)}, bf16[2,1152,3,144]{1,3,2,0:T(8,128)(2,1)}, bf16[2,144,1152]{2,1,0:T(8,128)(2,1)}, bf1...) async-done(((bf16[2,144,6912]{2,1,0:T(8,128)(2,1)}, bf16[2,1152,3,144]{1,3,2,0:T(8,128)(2,1)}, bf16[2,144,1152]{2,1,0:T(8,128)(2,1)}, bf16[2,1152,576]{1,2,0:T(8,128)(2,1)}, ...) | async-done | bytes 11943952 | tf_op jit(solution)/shard_map/psum | solution.py:310
  1336.2 2.2 convert_element_type.435
  1338.4 6.0 convert_element_type.427
  1344.5 2.2 convert_element_type.429
  1347.5 2.7 convert_element_type.439
  1350.4 2.7 convert_element_type.443
  (423 shorter events, 100.0 us)
Async XLA Ops:
  7.2 89.7 %all-gather.9.cloned.1.call-start = ((), (), s32[]{:S(2)}) async-start(), calls=%async_computation.8 | async-start | bytes 5308416 | tf_op jit(solution)/shard_map/all_gather | solution.py:90
  7.9 6.0 copy-start.105
  9.1 36.5 %copy-start.66 = (f32[256]{0:T(256)}, f32[256]{0:T(256)S(1)}, u32[]{:S(2)}) copy-start(f32[256]{0:T(256)S(1)} %broadcast_multiply_fusion.3) | copy-start | bytes 3076
  10.5 35.1 %copy-start.78 = (f32[256]{0:T(256)}, f32[256]{0:T(256)S(1)}, u32[]{:S(2)}) copy-start(f32[256]{0:T(256)S(1)} %fusion.137) | copy-start | bytes 3076
  11.1 33.7 %copy-start.68 = (bf16[2,6912]{1,0:T(2,128)(2,1)S(1)}, bf16[2,6912]{1,0:T(2,128)(2,1)}, u32[]{:S(2)}) copy-start(bf16[2,6912]{1,0:T(2,128)(2,1)} %param.16) | copy-start | bytes 82948
  11.1 34.5 %copy-start = (bf16[1,256,1152]{2,1,0:T(8,128)(2,1)S(1)}, bf16[1,256,1152]{2,1,0:T(8,128)(2,1)}, u32[]{:S(2)}) copy-start(bf16[1,256,1152]{2,1,0:T(8,128)(2,1)} %param.13) | copy-start | bytes 1769476
  13.9 32.9 %copy-start.107 = (bf16[2,2,144]{2,1,0:T(2,128)(2,1)S(1)}, bf16[2,2,144]{2,1,0:T(2,128)(2,1)}, u32[]{:S(2)}) copy-start(bf16[2,2,144]{2,1,0:T(2,128)(2,1)} %param.18) | copy-start | bytes 3460
  13.9 32.9 %copy-start.30 = (bf16[2,1152,3,144]{1,3,2,0:T(8,128)(2,1)S(1)}, bf16[2,1152,3,144]{1,3,2,0:T(8,128)(2,1)}, u32[]{:S(2)}) copy-start(bf16[2,1152,3,144]{1,3,2,0:T(8,128)(2,1)} %param.17) | copy-start | bytes 5971972
  45.6 125.8 %copy-start.54 = (f32[1152]{0:T(1024)}, f32[1152]{0:T(1024)S(1)}, u32[]{:S(2)}) copy-start(f32[1152]{0:T(1024)S(1)} %get-tuple-element.30) | copy-start | bytes 13828
  45.6 245.9 %copy-start.59 = (f32[1152]{0:T(1024)}, f32[1152]{0:T(1024)S(1)}, u32[]{:S(2)}) copy-start(f32[1152]{0:T(1024)S(1)} %get-tuple-element.31) | copy-start | bytes 13828
  45.6 247.8 %copy-start.48 = (f32[1152]{0:T(1024)}, f32[1152]{0:T(1024)S(1)}, u32[]{:S(2)}) copy-start(f32[1152]{0:T(1024)S(1)} %get-tuple-element.27) | copy-start | bytes 13828
  46.8 121.7 %reduce-scatter.9.cloned.1.call-start = ((), (), s32[]{:S(2)}) async-start(), calls=%async_computation.9 | async-start | bytes 5308416 | tf_op jit(solution)/shard_map/reduce_scatter | solution.py:94
  114.6 108.4 %all-gather.11.cloned.1.call-start = ((), (), s32[]{:S(2)}) async-start(), calls=%async_computation.10 | async-start | bytes 5308416 | tf_op jit(solution)/shard_map/all_gather | solution.py:90
  169.9 58.7 %copy-start.69 = (f32[256]{0:T(256)}, f32[256]{0:T(256)S(1)}, u32[]{:S(2)}) copy-start(f32[256]{0:T(256)S(1)} %broadcast_multiply_fusion.2) | copy-start | bytes 3076
  171.4 57.2 %copy-start.101 = (f32[256]{0:T(256)}, f32[256]{0:T(256)S(1)}, u32[]{:S(2)}) copy-start(f32[256]{0:T(256)S(1)} %multiply_reduce_fusion.9) | copy-start | bytes 3076
  171.4 57.2 %copy-start.80 = (f32[256]{0:T(256)}, f32[256]{0:T(256)S(1)}, u32[]{:S(2)}) copy-start(f32[256]{0:T(256)S(1)} %fusion.138) | copy-start | bytes 3076
  172.7 118.8 %reduce-scatter.11.cloned.1.call-start = ((), (), s32[]{:S(2)}) async-start(), calls=%async_computation.11 | async-start | bytes 5308416 | tf_op jit(solution)/shard_map/reduce_scatter | solution.py:94
  173.6 55.0 %copy-start.109 = (f32[576]{0:T(1024)}, f32[576]{0:T(1024)S(1)}, u32[]{:S(2)}) copy-start(f32[576]{0:T(1024)S(1)} %get-tuple-element.40) | copy-start | bytes 6916
  223.0 7.9 copy-start.116
  237.6 107.1 %all-gather.13.cloned.1.call-start = ((), (), s32[]{:S(2)}) async-start(), calls=%async_computation.12 | async-start | bytes 5308416 | tf_op jit(solution)/shard_map/all_gather | solution.py:90
  238.9 55.6 %copy-start.57 = (f32[1152]{0:T(1024)}, f32[1152]{0:T(1024)S(1)}, u32[]{:S(2)}) copy-start(f32[1152]{0:T(1024)S(1)} %get-tuple-element.36) | copy-start | bytes 13828
  293.0 51.7 %copy-start.37 = (bf16[1,1152,3,144]{1,3,2,0:T(8,128)(2,1)S(1)}, bf16[1,1152,3,144]{1,3,2,0:T(8,128)(2,1)}, u32[]{:S(2)}) copy-start(bf16[1,1152,3,144]{1,3,2,0:T(8,128)(2,1)} %get-tuple-element.78) | copy-start | bytes 2985988
  293.1 56.5 %copy-start.64 = (f32[256]{0:T(256)}, f32[256]{0:T(256)S(1)}, u32[]{:S(2)}) copy-start(f32[256]{0:T(256)S(1)} %broadcast_multiply_fusion.1) | copy-start | bytes 3076
  293.3 56.2 %copy-start.103 = (f32[256]{0:T(256)}, f32[256]{0:T(256)S(1)}, u32[]{:S(2)}) copy-start(f32[256]{0:T(256)S(1)} %multiply_reduce_fusion.8) | copy-start | bytes 3076
  293.4 56.2 %copy-start.76 = (f32[256]{0:T(256)}, f32[256]{0:T(256)S(1)}, u32[]{:S(2)}) copy-start(f32[256]{0:T(256)S(1)} %fusion.139) | copy-start | bytes 3076
  294.5 132.8 %reduce-scatter.13.cloned.1.call-start = ((), (), s32[]{:S(2)}) async-start(), calls=%async_computation.13 | async-start | bytes 5308416 | tf_op jit(solution)/shard_map/reduce_scatter | solution.py:94
  373.4 108.7 %all-gather.15.cloned.1.call-start = ((), (), s32[]{:S(2)}) async-start(), calls=%async_computation.14 | async-start | bytes 5308416 | tf_op jit(solution)/shard_map/all_gather | solution.py:90
  431.9 103.0 %all-gather.17.cloned.1.call-start = ((), (), s32[]{:S(2)}) async-start(), calls=%async_computation.16 | async-start | bytes 5308416 | tf_op jit(solution)/shard_map/all_gather | solution.py:100
  434.5 171.4 %reduce-scatter.17.cloned.1.call-start = ((), (), s32[]{:S(2)}) async-start(), calls=%async_computation.17 | async-start | bytes 5308416 | tf_op jit(solution)/shard_map/reduce_scatter | solution.py:104
  534.8 11.3 copy-start.117
  552.0 110.0 %reduce-scatter.15.cloned.1.call-start = ((), (), s32[]{:S(2)}) async-start(), calls=%async_computation.15 | async-start | bytes 5308416 | tf_op jit(solution)/shard_map/reduce_scatter | solution.py:94
  562.3 155.4 %all-gather.19.cloned.1.call-start = ((), (), s32[]{:S(2)}) async-start(), calls=%async_computation.18 | async-start | bytes 5308416 | tf_op jit(solution)/shard_map/all_gather | solution.py:100
  664.7 53.0 %copy-start.41 = (bf16[2,144,1152]{2,1,0:T(8,128)(2,1)S(1)}, bf16[2,144,1152]{2,1,0:T(8,128)(2,1)}, u32[]{:S(2)}) copy-start(bf16[2,144,1152]{2,1,0:T(8,128)(2,1)} %param.19) | copy-start | bytes 1990660
  664.7 53.0 %copy-start.82 = (f32[256]{0:T(256)}, f32[256]{0:T(256)S(1)}, u32[]{:S(2)}) copy-start(f32[256]{0:T(256)S(1)} %negate_multiply_fusion.3) | copy-start | bytes 3076
  667.5 135.6 %reduce-scatter.19.cloned.1.call-start = ((), (), s32[]{:S(2)}) async-start(), calls=%async_computation.19 | async-start | bytes 5308416 | tf_op jit(solution)/shard_map/reduce_scatter | solution.py:104
  749.2 58.3 %copy-start.3 = (f32[256,1152]{1,0:T(8,128)S(1)}, f32[256,1152]{1,0:T(8,128)}, u32[]{:S(2)}) copy-start(f32[256,1152]{1,0:T(8,128)} %copy-done.2) | copy-start | bytes 3538948
  749.2 111.1 %all-gather.21.cloned.1.call-start = ((), (), s32[]{:S(2)}) async-start(), calls=%async_computation.20 | async-start | bytes 5308416 | tf_op jit(solution)/shard_map/all_gather | solution.py:100
  810.1 121.3 %reduce-scatter.21.cloned.1.call-start = ((), (), s32[]{:S(2)}) async-start(), calls=%async_computation.21 | async-start | bytes 5308416 | tf_op jit(solution)/shard_map/reduce_scatter | solution.py:104
  860.3 11.3 copy-start.118
  877.4 54.0 %copy-start.55 = (f32[1152]{0:T(1024)S(1)}, f32[1152]{0:T(1024)}, u32[]{:S(2)}) copy-start(f32[1152]{0:T(1024)} %copy-done.54) | copy-start | bytes 13828
  877.4 54.0 %copy-start.70 = (f32[256]{0:T(256)S(1)}, f32[256]{0:T(256)}, u32[]{:S(2)}) copy-start(f32[256]{0:T(256)} %copy-done.69) | copy-start | bytes 3076
  877.4 54.0 %copy-start.81 = (f32[256]{0:T(256)S(1)}, f32[256]{0:T(256)}, u32[]{:S(2)}) copy-start(f32[256]{0:T(256)} %copy-done.80) | copy-start | bytes 3076
  877.4 56.3 %copy-start.102 = (f32[256]{0:T(256)S(1)}, f32[256]{0:T(256)}, u32[]{:S(2)}) copy-start(f32[256]{0:T(256)} %copy-done.101) | copy-start | bytes 3076
  877.5 56.9 %copy-start.7 = (f32[256,1152]{1,0:T(8,128)S(1)}, f32[256,1152]{1,0:T(8,128)}, u32[]{:S(2)}) copy-start(f32[256,1152]{1,0:T(8,128)} %get-tuple-element.58) | copy-start | bytes 3538948
  877.5 109.3 %all-gather.23.cloned.1.call-start = ((), (), s32[]{:S(2)}) async-start(), calls=%async_computation.22 | async-start | bytes 5308416 | tf_op jit(solution)/shard_map/all_gather | solution.py:100
  934.4 52.4 %copy-start.42 = (bf16[2,144,1152]{2,1,0:T(8,128)(2,1)S(1)}, bf16[2,144,1152]{2,1,0:T(8,128)(2,1)}, u32[]{:S(2)}) copy-start(bf16[2,144,1152]{2,1,0:T(8,128)(2,1)} %param.19) | copy-start | bytes 1990660
  936.5 54.5 %copy-start.63 = (f32[8,2,256]{2,1,0:T(2,128)S(1)}, f32[8,2,256]{2,1,0:T(2,128)}, u32[]{:S(2)}) copy-start(f32[8,2,256]{2,1,0:T(2,128)} %copy-done.62) | copy-start | bytes 49156
  936.5 130.9 %reduce-scatter.23.cloned.1.call-start = ((), (), s32[]{:S(2)}) async-start(), calls=%async_computation.23 | async-start | bytes 5308416 | tf_op jit(solution)/shard_map/reduce_scatter | solution.py:104
  1003.8 332.4 %all-reduce.5.cloned.1.call-start = ((), (), s32[]{:S(2)}) async-start(), calls=%async_computation.24 | async-start | bytes 23887872 | tf_op jit(solution)/shard_map/psum | solution.py:310
  1005.0 7.3 copy-start.111
  1012.4 9.2 copy-start.93
  1012.4 11.6 copy-start.4
  1012.4 11.6 copy-start.56
  1030.1 6.3 copy-start.87
  1030.1 6.5 copy-start.91
  1030.1 6.8 copy-start.90
  1030.1 7.1 copy-start.85
  1030.2 7.3 copy-start.89
  1030.2 7.8 copy-start.28
  1030.2 7.8 copy-start.58
  1038.2 6.5 copy-start.33
  1046.4 8.2 copy-start.32
  1070.9 30.2 %copy-start.108 = (f32[144]{0:T(256)S(1)}, f32[144]{0:T(256)}, u32[]{:S(2)}) copy-start(f32[144]{0:T(256)} %get-tuple-element.54) | copy-start | bytes 1732
  1338.4 6.0 copy-start.31
  (77 other events, 201.4 us)
Sparse Core Ops, SparseCore 0:
  46.9 49.9 all-gather.8
  114.7 53.7 reduce-scatter.8
  172.9 50.0 all-gather.10
  237.7 53.7 reduce-scatter.10
  294.6 50.0 all-gather.12
  373.5 53.7 reduce-scatter.12
  432.0 50.0 all-gather.14
  484.3 50.5 all-gather.16
  552.1 53.7 reduce-scatter.16
  608.7 53.3 reduce-scatter.14
  667.6 50.0 all-gather.18
  749.3 53.7 reduce-scatter.18
  810.2 50.0 all-gather.20
  877.6 53.7 reduce-scatter.20
  936.6 50.0 all-gather.22
  1003.9 53.7 reduce-scatter.22
  1103.7 232.4 all-reduce.4
where the time goes:
time: 1370 us; the launch traced here: 1360 us
  waiting for transfers between devices  959 us (70%)
  matrix products  176 us (13%)
  other arithmetic  82.1 us (6%)
  blocking collectives  76 us (6%)
  local copies, waits for them, and re-layouts  48.3 us (4%)
  between operations  16 us (1%)
    reduce_scatter x4, waiting for transfers between devices, reduce_rows(): lax.psum_scatter(partial_terms.astype(jnp.bfloat16), 'tensor', scatter_di...  212 us
    psum x1, waiting for transfers between devices, per_device(): lax.psum(ada_w_grad.astype(jnp.bfloat16), 'dp').astype(jnp.float32)  206 us
    all_gather x4, waiting for transfers between devices, spread_rows(): return lax.all_gather(row_block, 'tensor', axis=0, tiled=True)  195 us
    all_gather x4, waiting for transfers between devices, spread_grads(): return lax.all_gather(row_block, 'tensor', axis=0, tiled=True)  194 us
    reduce_scatter x4, waiting for transfers between devices, reduce_grads(): lax.psum_scatter(partial_terms.astype(jnp.bfloat16), 'tensor', scatter_di...  151 us
    psum x1, blocking collectives, per_device(): modulations = lax.psum(ada_terms, 'tensor') + ada_bias.astype(jnp.float32)  30.9 us
    unnamed x278, local copies, waits for them, and re-layouts  27.9 us
  transfers between devices with their start and end apart: 17, of which 16 were waited for; matrix products, arithmetic and copies ran while one was open for 7% of the time, Pallas kernels for 0%

commit v1 on v0

--- a/solution.py
+++ b/solution.py
@@ -307,7 +307,7 @@
     silu_grad = jnp.einsum("lm,ldm->d", mod_low, ada_weight, preferred_element_type=jnp.float32)
     cond_grad = silu_back(silu_grad)[0]
     summed = (
-        lax.psum(ada_w_grad.astype(jnp.bfloat16), "dp").astype(jnp.float32),
+        jnp.sum(lax.all_gather(ada_w_grad.astype(jnp.bfloat16), "dp"), axis=0).astype(jnp.float32),
         lax.psum(ada_b_grad.astype(jnp.bfloat16), "dp").astype(jnp.float32),
         lax.psum(collect(0).astype(jnp.bfloat16), "dp").astype(jnp.float32),
         lax.psum(collect(1).astype(jnp.bfloat16), "dp").astype(jnp.float32),

time: 1370 us -> 1410 us (1.029)
  waiting for transfers between devices: 959 us -> 1000 us
  matrix products: 176 us -> 156 us
  other arithmetic: 82.1 us -> 96.7 us
    all_gather x0 -> x1, waiting for transfers between devices: none -> 119 us  [per_device(): lax.all_gather(ada_w_grad.astype(jnp.bfloat16), 'dp')]
    psum x1, waiting for transfers between devices: 206 us -> 128 us  [per_device(): lax.psum(collect(0).astype(jnp.bfloat16), 'dp').astype(jnp.float32)]
    unnamed x278 -> x274, local copies, waits for them, and re-layouts: 27.9 us -> 33.1 us
  transfers between devices with their start and end apart: 17 -> 18, of which waited for: 16 -> 17; matrix products, arithmetic and copies ran while one was open for 7% -> 8% of each run, Pallas kernels for 0% -> 0%
where the time goes in v1:
time: 1410 us; the launch traced here: 1400 us
  waiting for transfers between devices  1000 us (71%)
  matrix products  156 us (11%)
  other arithmetic  96.7 us (7%)
  blocking collectives  75.8 us (5%)
  local copies, waits for them, and re-layouts  57.3 us (4%)
  between operations  16.3 us (1%)
    reduce_scatter x4, waiting for transfers between devices, reduce_rows(): lax.psum_scatter(partial_terms.astype(jnp.bfloat16), 'tensor', scatter_di...  212 us
    all_gather x4, waiting for transfers between devices, spread_rows(): return lax.all_gather(row_block, 'tensor', axis=0, tiled=True)  195 us
    all_gather x4, waiting for transfers between devices, spread_grads(): return lax.all_gather(row_block, 'tensor', axis=0, tiled=True)  194 us
    reduce_scatter x4, waiting for transfers between devices, reduce_grads(): lax.psum_scatter(partial_terms.astype(jnp.bfloat16), 'tensor', scatter_di...  151 us
    psum x1, waiting for transfers between devices, per_device(): lax.psum(collect(0).astype(jnp.bfloat16), 'dp').astype(jnp.float32)  128 us
    all_gather x1, waiting for transfers between devices, per_device(): lax.all_gather(ada_w_grad.astype(jnp.bfloat16), 'dp')  119 us
    unnamed x274, local copies, waits for them, and re-layouts  33.1 us
    psum x1, blocking collectives, per_device(): modulations = lax.psum(ada_terms, 'tensor') + ada_bias.astype(jnp.float32)  30.9 us
  transfers between devices with their start and end apart: 18, of which 17 were waited for; matrix products, arithmetic and copies ran while one was open for 8% of the time, Pallas kernels for 0%

profile of v1, /device:TPU:0, one launch (start us, length us, event | category | flops | bytes accessed | tf_op | source)
XLA Modules:
  0.0 1404.6 jit_solution(7734177035820186794)
XLA Ops:
  11.1 2.8 fusion.180
  14.0 30.9 %psum.91 = f32[2,6912]{1,0:T(2,128)S(1)} all-reduce(f32[2,6912]{1,0:T(2,128)S(1)} %bitcast.364), channel_id=1, replica_groups=mesh['dp'=4,'tensor'=8] {'tensor'}, use_global_device_ids=true, to_apply=%region_0.1 | all-reduce | flops 13824 | bytes 110592 | tf_op jit(solution)/shard_map/psum | solution.py:263
  48.3 48.5 %all-gather.10.cloned.1.call-done = bf16[2048,1152]{1,0:T(8,128)(2,1)} async-done(((bf16[256,1152]{1,0:T(8,128)(2,1)}), bf16[2048,1152]{1,0:T(8,128)(2,1)}) %all-gather.10.cloned.1.call-update) | async-done | bytes 4718608 | tf_op jit(solution)/shard_map/all_gather | solution.py:90
  96.8 5.1 fusion.181
  104.4 3.2 fusion.168
  110.8 3.8 convolution_convert_fusion.7
  115.8 52.6 %reduce-scatter.9.cloned.1.call-done = bf16[256,1152]{1,0:T(8,128)(2,1)} async-done(((bf16[2048,1152]{1,0:T(8,128)(2,1)}), bf16[256,1152]{1,0:T(8,128)(2,1)}) %reduce-scatter.9.cloned.1.call-update) | async-done | bytes 589840 | tf_op jit(solution)/shard_map/reduce_scatter | solution.py:94
  173.6 49.3 %all-gather.12.cloned.1.call-done = bf16[2048,1152]{1,0:T(8,128)(2,1)} async-done(((bf16[256,1152]{1,0:T(8,128)(2,1)}), bf16[2048,1152]{1,0:T(8,128)(2,1)}) %all-gather.12.cloned.1.call-update) | async-done | bytes 4718608 | tf_op jit(solution)/shard_map/all_gather | solution.py:90
  223.0 5.6 fusion.59
  228.7 2.2 copy-done.106
  230.9 6.7 convolution_convert_fusion.6
  238.9 52.6 %reduce-scatter.11.cloned.1.call-done = bf16[256,1152]{1,0:T(8,128)(2,1)} async-done(((bf16[2048,1152]{1,0:T(8,128)(2,1)}), bf16[256,1152]{1,0:T(8,128)(2,1)}) %reduce-scatter.11.cloned.1.call-update) | async-done | bytes 589840 | tf_op jit(solution)/shard_map/reduce_scatter | solution.py:94
  294.6 50.2 %all-gather.14.cloned.1.call-done = bf16[2048,1152]{1,0:T(8,128)(2,1)} async-done(((bf16[256,1152]{1,0:T(8,128)(2,1)}), bf16[2048,1152]{1,0:T(8,128)(2,1)}) %all-gather.14.cloned.1.call-update) | async-done | bytes 4718608 | tf_op jit(solution)/shard_map/all_gather | solution.py:90
  344.7 4.8 fusion.182
  356.7 5.3 fusion.169
  362.0 3.7 fusion.40
  368.6 4.8 convolution_convert_fusion.5
  373.5 53.9 %reduce-scatter.13.cloned.1.call-done = bf16[256,1152]{1,0:T(8,128)(2,1)} async-done(((bf16[2048,1152]{1,0:T(8,128)(2,1)}), bf16[256,1152]{1,0:T(8,128)(2,1)}) %reduce-scatter.13.cloned.1.call-update) | async-done | bytes 589840 | tf_op jit(solution)/shard_map/reduce_scatter | solution.py:94
  431.9 2.6 fusion.159
  435.0 47.1 %all-gather.16.cloned.1.call-done = bf16[2048,1152]{1,0:T(8,128)(2,1)} async-done(((bf16[256,1152]{1,0:T(8,128)(2,1)}), bf16[2048,1152]{1,0:T(8,128)(2,1)}) %all-gather.16.cloned.1.call-update) | async-done | bytes 4718608 | tf_op jit(solution)/shard_map/all_gather | solution.py:90
  482.1 8.2 fusion.51
  490.3 44.6 %all-gather.18.cloned.1.call-done = bf16[2048,1152]{1,0:T(8,128)(2,1)} async-done(((bf16[256,1152]{1,0:T(8,128)(2,1)}), bf16[2048,1152]{1,0:T(8,128)(2,1)}) %all-gather.18.cloned.1.call-update) | async-done | bytes 4718608 | tf_op jit(solution)/shard_map/all_gather | solution.py:100
  534.9 9.9 fusion.178
  546.2 5.8 convolution_convert_fusion.3
  552.3 10.0 convolution_convert_fusion.4
  562.4 43.6 %reduce-scatter.17.cloned.1.call-done = bf16[256,1152]{1,0:T(8,128)(2,1)} async-done(((bf16[2048,1152]{1,0:T(8,128)(2,1)}), bf16[256,1152]{1,0:T(8,128)(2,1)}) %reduce-scatter.17.cloned.1.call-update) | async-done | bytes 589840 | tf_op jit(solution)/shard_map/reduce_scatter | solution.py:104
  609.3 52.7 %reduce-scatter.15.cloned.1.call-done = bf16[256,1152]{1,0:T(8,128)(2,1)} async-done(((bf16[2048,1152]{1,0:T(8,128)(2,1)}), bf16[256,1152]{1,0:T(8,128)(2,1)}) %reduce-scatter.15.cloned.1.call-update) | async-done | bytes 589840 | tf_op jit(solution)/shard_map/reduce_scatter | solution.py:94
  662.1 2.7 fusion.164
  667.8 49.9 %all-gather.20.cloned.1.call-done = bf16[2048,1152]{1,0:T(8,128)(2,1)} async-done(((bf16[256,1152]{1,0:T(8,128)(2,1)}), bf16[2048,1152]{1,0:T(8,128)(2,1)}) %all-gather.20.cloned.1.call-update) | async-done | bytes 4718608 | tf_op jit(solution)/shard_map/all_gather | solution.py:100
  717.7 4.0 convolution_convert_fusion.17
  723.7 4.2 fusion.174
  731.7 2.3 fusion.175
  744.5 4.6 convolution_convert_fusion.1
  749.2 53.9 %reduce-scatter.19.cloned.1.call-done = bf16[256,1152]{1,0:T(8,128)(2,1)} async-done(((bf16[2048,1152]{1,0:T(8,128)(2,1)}), bf16[256,1152]{1,0:T(8,128)(2,1)}) %reduce-scatter.19.cloned.1.call-update) | async-done | bytes 589840 | tf_op jit(solution)/shard_map/reduce_scatter | solution.py:104
  805.3 2.2 fusion.75
  807.6 2.5 fusion.158
  810.6 49.7 %all-gather.22.cloned.1.call-done = bf16[2048,1152]{1,0:T(8,128)(2,1)} async-done(((bf16[256,1152]{1,0:T(8,128)(2,1)}), bf16[2048,1152]{1,0:T(8,128)(2,1)}) %all-gather.22.cloned.1.call-update) | async-done | bytes 4718608 | tf_op jit(solution)/shard_map/all_gather | solution.py:100
  860.3 9.9 fusion.179
  870.1 5.8 convolution_convert_fusion.2
  876.1 53.9 %reduce-scatter.21.cloned.1.call-done = bf16[256,1152]{1,0:T(8,128)(2,1)} async-done(((bf16[2048,1152]{1,0:T(8,128)(2,1)}), bf16[256,1152]{1,0:T(8,128)(2,1)}) %reduce-scatter.21.cloned.1.call-update) | async-done | bytes 589840 | tf_op jit(solution)/shard_map/reduce_scatter | solution.py:104
  929.9 2.4 fusion.76
  935.1 50.2 %all-gather.24.cloned.1.call-done = bf16[2048,1152]{1,0:T(8,128)(2,1)} async-done(((bf16[256,1152]{1,0:T(8,128)(2,1)}), bf16[2048,1152]{1,0:T(8,128)(2,1)}) %all-gather.24.cloned.1.call-update) | async-done | bytes 4718608 | tf_op jit(solution)/shard_map/all_gather | solution.py:100
  985.3 4.1 convolution_convert_fusion.16
  997.7 4.6 convolution_convert_fusion
  1002.5 6.4 fusion.22
  1009.0 8.1 fusion.20
  1017.1 3.5 fusion.24
  1020.7 2.4 convolution_convert_fusion.12
  1023.2 3.2 fusion.21
  1028.3 4.5 fusion.19
  1036.4 2.5 convolution_convert_fusion.13
  1044.9 2.5 fusion.79
  1063.0 2.7 multiply_reduce_fusion.6
  1066.8 27.6 %all-reduce = (bf16[2,6912]{1,0:T(2,128)(2,1)S(1)}, bf16[2,1152]{1,0:T(2,128)(2,1)S(1)}, bf16[2,1152]{1,0:T(2,128)(2,1)S(1)}) all-reduce(bf16[2,6912]{1,0:T(2,128)(2,1)S(1)} %pad_maximum_fusion.4, bf16[2,1152]{1,0:T(2,128)(2,1)S(1)} %get-tuple-element.107, ...), channel_id=1, replica_groups=mesh['dp'=4,'tensor'=8] {'tensor'}, use_global_device_ids=true, to_apply=%region_43.44 | all-reduce | flops 18432 | bytes 73728 | tf_op jit(solution)/shard_map/psum | solution.py:298
  1094.4 2.5 multiply_convert_fusion
  1098.0 128.0 %all-reduce.5.cloned.1.call-done = (bf16[2,1152,3,144]{1,3,2,0:T(8,128)(2,1)}, bf16[2,144,1152]{2,1,0:T(8,128)(2,1)}, bf16[2,1152,576]{1,2,0:T(8,128)(2,1)}, bf16[2,576,1152]{2,1,0:T(8,128)(2,1)}) async-done(((bf16[2,1152,3,144]{1,3,2,0:T(8,128)(2,1)}, bf16[2,144,1152]{2,1,0:T(8,128)(2,1)}, bf16[2,1152,576]{1,2,0:T(8,128)(2,1)}, bf16[2,576,1152]{2,1,0:T(8,128)(2,1)}), (bf16[2,1152,3,144]{1,3,2,0:T(8,128)(2,1)}, ...) | async-done | bytes 7962640 | tf_op jit(solution)/shard_map/psum | solution.py:312
  1225.9 2.4 convert_element_type.444
  1228.3 2.2 convert_element_type.438
  1231.4 2.8 convert_element_type.448
  1234.2 3.4 convert_element_type.452
  1240.7 17.3 %all-reduce.1 = (bf16[2,6912]{1,0:T(2,128)(2,1)S(1)}, bf16[2,2,144]{2,1,0:T(2,128)(2,1)S(1)}, bf16[2,1152]{1,0:T(2,128)(2,1)S(1)}, bf16[2,576]{1,0:T(2,128)(2,1)S(1)}, bf16[2,1152]{1,0:T(2,128)(2,1)S(1)}) all-reduce(bf16[2,6912]{1,0:T(2,128)(2,1)S(1)} %get-tuple-element.41, ...), channel_id=1, replica_groups=mesh['dp'=4,'tensor'=8] {'dp'}, use_global_device_ids=true, to_apply=%region_45.46 | all-reduce | flops 20160 | bytes 80640 | tf_op jit(solution)/shard_map/psum | solution.py:311
  1261.0 118.9 %all-gather.26.cloned.1.call-done = bf16[4,2,144,6912]{3,2,1,0:T(8,128)(2,1)} async-done(((bf16[1,2,144,6912]{3,2,1,0:T(8,128)(2,1)}), bf16[4,2,144,6912]{3,2,1,0:T(8,128)(2,1)}) %all-gather.26.cloned.1.call-update) | async-done | bytes 15925264 | tf_op jit(solution)/shard_map/all_gather | solution.py:310
  1379.9 11.5 reduce_sum.436
  1391.4 5.9 convert_element_type.436
  (429 shorter events, 112.7 us)
Async XLA Ops:
  7.2 89.7 %all-gather.10.cloned.1.call-start = ((), (), s32[]{:S(2)}) async-start(), calls=%async_computation.8 | async-start | bytes 5308416 | tf_op jit(solution)/shard_map/all_gather | solution.py:90
  9.1 36.5 %copy-start.61 = (f32[256]{0:T(256)}, f32[256]{0:T(256)S(1)}, u32[]{:S(2)}) copy-start(f32[256]{0:T(256)S(1)} %broadcast_multiply_fusion.3) | copy-start | bytes 3076
  10.5 35.1 %copy-start.73 = (f32[256]{0:T(256)}, f32[256]{0:T(256)S(1)}, u32[]{:S(2)}) copy-start(f32[256]{0:T(256)S(1)} %fusion.137) | copy-start | bytes 3076
  11.1 33.7 %copy-start.63 = (bf16[2,6912]{1,0:T(2,128)(2,1)S(1)}, bf16[2,6912]{1,0:T(2,128)(2,1)}, u32[]{:S(2)}) copy-start(bf16[2,6912]{1,0:T(2,128)(2,1)} %param.16) | copy-start | bytes 82948
  11.1 34.5 %copy-start = (bf16[1,256,1152]{2,1,0:T(8,128)(2,1)S(1)}, bf16[1,256,1152]{2,1,0:T(8,128)(2,1)}, u32[]{:S(2)}) copy-start(bf16[1,256,1152]{2,1,0:T(8,128)(2,1)} %param.13) | copy-start | bytes 1769476
  13.9 32.9 %copy-start.92 = (bf16[2,2,144]{2,1,0:T(2,128)(2,1)S(1)}, bf16[2,2,144]{2,1,0:T(2,128)(2,1)}, u32[]{:S(2)}) copy-start(bf16[2,2,144]{2,1,0:T(2,128)(2,1)} %param.18) | copy-start | bytes 3460
  13.9 32.9 %copy-start.29 = (bf16[2,1152,3,144]{1,3,2,0:T(8,128)(2,1)S(1)}, bf16[2,1152,3,144]{1,3,2,0:T(8,128)(2,1)}, u32[]{:S(2)}) copy-start(bf16[2,1152,3,144]{1,3,2,0:T(8,128)(2,1)} %param.17) | copy-start | bytes 5971972
  45.6 125.9 %copy-start.50 = (f32[1152]{0:T(1024)}, f32[1152]{0:T(1024)S(1)}, u32[]{:S(2)}) copy-start(f32[1152]{0:T(1024)S(1)} %get-tuple-element.30) | copy-start | bytes 13828
  45.6 245.9 %copy-start.54 = (f32[1152]{0:T(1024)}, f32[1152]{0:T(1024)S(1)}, u32[]{:S(2)}) copy-start(f32[1152]{0:T(1024)S(1)} %get-tuple-element.31) | copy-start | bytes 13828
  45.6 247.8 %copy-start.44 = (f32[1152]{0:T(1024)}, f32[1152]{0:T(1024)S(1)}, u32[]{:S(2)}) copy-start(f32[1152]{0:T(1024)S(1)} %get-tuple-element.27) | copy-start | bytes 13828
  46.8 121.7 %reduce-scatter.9.cloned.1.call-start = ((), (), s32[]{:S(2)}) async-start(), calls=%async_computation.9 | async-start | bytes 5308416 | tf_op jit(solution)/shard_map/reduce_scatter | solution.py:94
  114.6 108.4 %all-gather.12.cloned.1.call-start = ((), (), s32[]{:S(2)}) async-start(), calls=%async_computation.10 | async-start | bytes 5308416 | tf_op jit(solution)/shard_map/all_gather | solution.py:90
  170.0 58.7 %copy-start.64 = (f32[256]{0:T(256)}, f32[256]{0:T(256)S(1)}, u32[]{:S(2)}) copy-start(f32[256]{0:T(256)S(1)} %broadcast_multiply_fusion.2) | copy-start | bytes 3076
  171.4 57.2 %copy-start.86 = (f32[256]{0:T(256)}, f32[256]{0:T(256)S(1)}, u32[]{:S(2)}) copy-start(f32[256]{0:T(256)S(1)} %multiply_reduce_fusion.9) | copy-start | bytes 3076
  171.4 57.2 %copy-start.75 = (f32[256]{0:T(256)}, f32[256]{0:T(256)S(1)}, u32[]{:S(2)}) copy-start(f32[256]{0:T(256)S(1)} %fusion.138) | copy-start | bytes 3076
  172.7 118.8 %reduce-scatter.11.cloned.1.call-start = ((), (), s32[]{:S(2)}) async-start(), calls=%async_computation.11 | async-start | bytes 5308416 | tf_op jit(solution)/shard_map/reduce_scatter | solution.py:94
  173.6 55.0 %copy-start.94 = (f32[576]{0:T(1024)}, f32[576]{0:T(1024)S(1)}, u32[]{:S(2)}) copy-start(f32[576]{0:T(1024)S(1)} %get-tuple-element.40) | copy-start | bytes 6916
  223.0 7.9 copy-start.101
  237.6 107.1 %all-gather.14.cloned.1.call-start = ((), (), s32[]{:S(2)}) async-start(), calls=%async_computation.12 | async-start | bytes 5308416 | tf_op jit(solution)/shard_map/all_gather | solution.py:90
  238.9 55.6 %copy-start.53 = (f32[1152]{0:T(1024)}, f32[1152]{0:T(1024)S(1)}, u32[]{:S(2)}) copy-start(f32[1152]{0:T(1024)S(1)} %get-tuple-element.36) | copy-start | bytes 13828
  293.1 51.7 %copy-start.34 = (bf16[1,1152,3,144]{1,3,2,0:T(8,128)(2,1)S(1)}, bf16[1,1152,3,144]{1,3,2,0:T(8,128)(2,1)}, u32[]{:S(2)}) copy-start(bf16[1,1152,3,144]{1,3,2,0:T(8,128)(2,1)} %get-tuple-element.77) | copy-start | bytes 2985988
  293.1 56.5 %copy-start.59 = (f32[256]{0:T(256)}, f32[256]{0:T(256)S(1)}, u32[]{:S(2)}) copy-start(f32[256]{0:T(256)S(1)} %broadcast_multiply_fusion.1) | copy-start | bytes 3076
  293.4 56.2 %copy-start.88 = (f32[256]{0:T(256)}, f32[256]{0:T(256)S(1)}, u32[]{:S(2)}) copy-start(f32[256]{0:T(256)S(1)} %multiply_reduce_fusion.8) | copy-start | bytes 3076
  293.4 56.2 %copy-start.71 = (f32[256]{0:T(256)}, f32[256]{0:T(256)S(1)}, u32[]{:S(2)}) copy-start(f32[256]{0:T(256)S(1)} %fusion.139) | copy-start | bytes 3076
  294.5 132.8 %reduce-scatter.13.cloned.1.call-start = ((), (), s32[]{:S(2)}) async-start(), calls=%async_computation.13 | async-start | bytes 5308416 | tf_op jit(solution)/shard_map/reduce_scatter | solution.py:94
  373.4 108.7 %all-gather.16.cloned.1.call-start = ((), (), s32[]{:S(2)}) async-start(), calls=%async_computation.14 | async-start | bytes 5308416 | tf_op jit(solution)/shard_map/all_gather | solution.py:90
  431.9 103.0 %all-gather.18.cloned.1.call-start = ((), (), s32[]{:S(2)}) async-start(), calls=%async_computation.16 | async-start | bytes 5308416 | tf_op jit(solution)/shard_map/all_gather | solution.py:100
  434.6 171.4 %reduce-scatter.17.cloned.1.call-start = ((), (), s32[]{:S(2)}) async-start(), calls=%async_computation.17 | async-start | bytes 5308416 | tf_op jit(solution)/shard_map/reduce_scatter | solution.py:104
  534.9 11.3 copy-start.102
  552.1 110.0 %reduce-scatter.15.cloned.1.call-start = ((), (), s32[]{:S(2)}) async-start(), calls=%async_computation.15 | async-start | bytes 5308416 | tf_op jit(solution)/shard_map/reduce_scatter | solution.py:94
  562.3 155.4 %all-gather.20.cloned.1.call-start = ((), (), s32[]{:S(2)}) async-start(), calls=%async_computation.18 | async-start | bytes 5308416 | tf_op jit(solution)/shard_map/all_gather | solution.py:100
  664.8 53.0 %copy-start.37 = (bf16[2,144,1152]{2,1,0:T(8,128)(2,1)S(1)}, bf16[2,144,1152]{2,1,0:T(8,128)(2,1)}, u32[]{:S(2)}) copy-start(bf16[2,144,1152]{2,1,0:T(8,128)(2,1)} %param.19) | copy-start | bytes 1990660
  664.8 53.0 %copy-start.77 = (f32[256]{0:T(256)}, f32[256]{0:T(256)S(1)}, u32[]{:S(2)}) copy-start(f32[256]{0:T(256)S(1)} %negate_multiply_fusion.3) | copy-start | bytes 3076
  667.5 135.6 %reduce-scatter.19.cloned.1.call-start = ((), (), s32[]{:S(2)}) async-start(), calls=%async_computation.19 | async-start | bytes 5308416 | tf_op jit(solution)/shard_map/reduce_scatter | solution.py:104
  749.2 58.3 %copy-start.3 = (f32[256,1152]{1,0:T(8,128)S(1)}, f32[256,1152]{1,0:T(8,128)}, u32[]{:S(2)}) copy-start(f32[256,1152]{1,0:T(8,128)} %copy-done.2) | copy-start | bytes 3538948
  749.2 111.1 %all-gather.22.cloned.1.call-start = ((), (), s32[]{:S(2)}) async-start(), calls=%async_computation.20 | async-start | bytes 5308416 | tf_op jit(solution)/shard_map/all_gather | solution.py:100
  810.1 119.9 %reduce-scatter.21.cloned.1.call-start = ((), (), s32[]{:S(2)}) async-start(), calls=%async_computation.21 | async-start | bytes 5308416 | tf_op jit(solution)/shard_map/reduce_scatter | solution.py:104
  860.3 9.9 copy-start.103
  876.0 54.0 %copy-start.51 = (f32[1152]{0:T(1024)S(1)}, f32[1152]{0:T(1024)}, u32[]{:S(2)}) copy-start(f32[1152]{0:T(1024)} %copy-done.50) | copy-start | bytes 13828
  876.0 54.0 %copy-start.65 = (f32[256]{0:T(256)S(1)}, f32[256]{0:T(256)}, u32[]{:S(2)}) copy-start(f32[256]{0:T(256)} %copy-done.64) | copy-start | bytes 3076
  876.0 54.0 %copy-start.76 = (f32[256]{0:T(256)S(1)}, f32[256]{0:T(256)}, u32[]{:S(2)}) copy-start(f32[256]{0:T(256)} %copy-done.75) | copy-start | bytes 3076
  876.0 56.3 %copy-start.87 = (f32[256]{0:T(256)S(1)}, f32[256]{0:T(256)}, u32[]{:S(2)}) copy-start(f32[256]{0:T(256)} %copy-done.86) | copy-start | bytes 3076
  876.0 56.9 %copy-start.8 = (f32[256,1152]{1,0:T(8,128)S(1)}, f32[256,1152]{1,0:T(8,128)}, u32[]{:S(2)}) copy-start(f32[256,1152]{1,0:T(8,128)} %get-tuple-element.57) | copy-start | bytes 3538948
  876.0 109.3 %all-gather.24.cloned.1.call-start = ((), (), s32[]{:S(2)}) async-start(), calls=%async_computation.22 | async-start | bytes 5308416 | tf_op jit(solution)/shard_map/all_gather | solution.py:100
  932.9 52.3 %copy-start.38 = (bf16[2,144,1152]{2,1,0:T(8,128)(2,1)S(1)}, bf16[2,144,1152]{2,1,0:T(8,128)(2,1)}, u32[]{:S(2)}) copy-start(bf16[2,144,1152]{2,1,0:T(8,128)(2,1)} %param.19) | copy-start | bytes 1990660
  935.1 54.5 %copy-start.58 = (f32[8,2,256]{2,1,0:T(2,128)S(1)}, f32[8,2,256]{2,1,0:T(2,128)}, u32[]{:S(2)}) copy-start(f32[8,2,256]{2,1,0:T(2,128)} %copy-done.57) | copy-start | bytes 49156
  935.1 124.0 %reduce-scatter.23.cloned.1.call-start = ((), (), s32[]{:S(2)}) async-start(), calls=%async_computation.23 | async-start | bytes 5308416 | tf_op jit(solution)/shard_map/reduce_scatter | solution.py:104
  1002.3 223.6 %all-reduce.5.cloned.1.call-start = ((), (), s32[]{:S(2)}) async-start(), calls=%async_computation.25 | async-start | bytes 15925248 | tf_op jit(solution)/shard_map/psum | solution.py:312
  1002.5 18.1 %slice-start.6 = ((s8[4718592]{0:T(1024)(128)(4,1)}), s8[4194304]{0:T(1024)(128)(4,1)S(1)}, s32[]{:S(2)}) async-start(s8[4718592]{0:T(1024)(128)(4,1)} %bitcast.376), calls=%async_computation.32 | async-start | bytes 8388608
  1009.0 8.1 copy-start.15
  1009.0 11.7 slice-start.7
  1020.7 7.6 slice-start.8
  1020.7 7.5 slice-start.10
  1026.4 8.1 slice-start
  1026.4 10.0 slice-start.2
  1028.3 8.1 slice-start.3
  1040.4 339.5 %all-gather.26.cloned.1.call-start = ((), (), s32[]{:S(2)}) async-start(), calls=%async_computation.24 | async-start | bytes 19906560 | tf_op jit(solution)/shard_map/all_gather | solution.py:310
  1047.4 11.4 copy-start.22
  1047.4 11.6 copy-start.69
  1047.5 11.6 copy-start.70
  1047.5 12.9 copy-start.82
  1047.5 13.2 copy-start.43
  1047.5 13.2 copy-start.62
  1062.7 31.7 %copy-start.93 = (f32[144]{0:T(256)S(1)}, f32[144]{0:T(256)}, u32[]{:S(2)}) copy-start(f32[144]{0:T(256)} %get-tuple-element.53) | copy-start | bytes 1732
  (76 other events, 215.3 us)
Sparse Core Ops, SparseCore 0:
  46.9 49.9 all-gather.9
  114.7 53.7 reduce-scatter.8
  172.9 50.0 all-gather.11
  237.7 53.7 reduce-scatter.10
  294.6 50.0 all-gather.13
  373.5 53.7 reduce-scatter.12
  432.0 50.0 all-gather.15
  484.3 50.5 all-gather.17
  552.2 53.7 reduce-scatter.16
  608.7 53.3 reduce-scatter.14
  667.6 50.0 all-gather.19
  749.3 53.7 reduce-scatter.18
  810.2 50.0 all-gather.21
  876.1 53.7 reduce-scatter.20
  935.2 50.0 all-gather.23
  1002.4 53.7 reduce-scatter.22
  1061.2 164.7 all-reduce.4
  1228.4 151.5 all-gather.25
